TPU v7x, 768 devices: a whole 4x8x12 slice. The times are simulated.
768 devices in a mesh: wide: 32 (over x_lo, y, core), narrow: 24 (over z, x_hi).
Axes of the slice: x: 4 (x_hi: 2, x_lo: 2; x = x_hi * 2 + x_lo), y: 8, z: 12, core: 2. Of those that a mesh axis runs over, the one named last changes fastest.
Arguments:
- weights: bfloat16 [32, 3072, 384], P('wide'), may hold values from -0.1875 to 0.1875
- act_rows: bfloat16 [32, 24, 1, 720, 1024], P('wide', 'narrow'), may hold values from -6 to 6
- grad_rows: bfloat16 [32, 24, 1, 720, 1024], P('wide', 'narrow'), may hold values from -6 to 6
- row_owner: int32 [32, 24, 720], P('wide', 'narrow'), may hold values from 0 to 31, as said below
- row_slot: int32 [32, 24, 720], P('wide', 'narrow'), may hold values from 0 to 29, as said below
- slot_token: int32 [32, 24, 960], P('wide', 'narrow'), may hold values from -1 to 127, as said below
- moment_one: float32 [32, 3072, 384], P('wide', 'narrow'), may hold values from -4 to 4
- moment_two: float32 [32, 3072, 384], P('wide', 'narrow'), may hold values from 0.3 to 3
Outputs:
- token_grads: bfloat16 [32, 24, 128, 1024], P('wide', 'narrow')
- new_weights: bfloat16 [32, 3072, 384], P('wide', 'narrow')
- new_one: float32 [32, 3072, 384], P('wide', 'narrow')
- new_two: float32 [32, 3072, 384], P('wide', 'narrow')
Inputs may be any that keep to these rules, and one draw needn't show every extreme that they name: `row_owner`: each device sends 30 rows to half of the owners and 15 rows to the other half; for every narrow index some owner receives 30 rows from every source. `row_slot`: the slots that one device uses for one owner are 0 up to the number of its rows for that owner minus 1, each once. `slot_token`: entry w * 30 + s at owner (o, n) is the owned token of the row that device (w, n) sends to o in slot s, and -1 exactly for the slots that device leaves empty.
All inputs are finite; a program needn't handle non-finite values.
Results may differ from a plain program's by a relative error of at most 0.01.
Values may be sent and summed in bfloat16 or wider, within the bound.
No kernel may reach another device: no remote copies, remote signals or barrier semaphores. Data moves between devices by JAX's collectives and lax.ppermute only.
A program may use at most 32 MiB of HBM per device.

v0:
```python
import math

import jax
import jax.numpy as jnp
from jax import lax
from jax.experimental import pallas as pl
from jax.experimental.pallas import tpu as pltpu
from jax.sharding import PartitionSpec as P

BETA_ONE = 0.9
BETA_TWO = 0.95
LEARN_RATE = 0.003
WEIGHT_DECAY = 0.1
EPSILON = 1e-08
CORR_ONE = 1.0 - 0.9**10
CORR_TWO = 1.0 - 0.95**10

FRAME = 32
LANES = 128

AHEAD, BEHIND, FAR, KEPT = (5, 3, 1), (-5, -3, -1), (6,), (4, -4, 2, -2, 0)
GROUPS = (AHEAD, BEHIND, FAR, *((offset,) for offset in KEPT))


def expert_kernel(narrow_ref, wide_ref, owner_ref, slot_ref, x_hbm, dy_hbm, w_hbm, *refs):
    targets, out_hbm = refs[: len(GROUPS)], refs[len(GROUPS)]
    x, dy, w, pair, hidden, terms, turned, out, in_sem, out_sem = refs[len(GROUPS) + 1 :]
    width, units = x.shape[1], w.shape[1]
    loads = [
        pltpu.make_async_copy(x_hbm, x, in_sem.at[0]),
        pltpu.make_async_copy(w_hbm.at[pl.ds(0, width)], w.at[pl.ds(0, width)], in_sem.at[1]),
        pltpu.make_async_copy(w_hbm.at[pl.ds(width, width)], w.at[pl.ds(width, width)], in_sem.at[2]),
        pltpu.make_async_copy(dy_hbm, dy, in_sem.at[3]),
        pltpu.make_async_copy(w_hbm.at[pl.ds(2 * width, width)], w.at[pl.ds(2 * width, width)], in_sem.at[4]),
    ]
    for load in loads:
        load.start()
    loads[0].wait()
    loads[1].wait()
    gate = jnp.dot(x[...], w[:width, :], preferred_element_type=jnp.float32)
    loads[2].wait()
    up = jnp.dot(x[...], w[width : 2 * width, :], preferred_element_type=jnp.float32)
    loads[3].wait()
    loads[4].wait()
    d_hidden = jnp.dot(dy[...], w[2 * width :, :], preferred_element_type=jnp.float32)
    prob = jax.nn.sigmoid(gate)
    active = gate * prob
    hidden[...] = (active * up).astype(jnp.bfloat16)
    pair[:, units:] = (d_hidden * active).astype(jnp.bfloat16)
    pair[:, :units] = (d_hidden * up * prob * (1.0 + gate * (1.0 - prob))).astype(jnp.bfloat16)
    sends = []

    ring = terms.shape[0]
    per = width // LANES
    first = (((0,), (0,)), ((), ()))
    for index, (left, right) in enumerate(((pair.at[:, :units], x), (pair.at[:, units:], x), (hidden, dy))):
        product = lax.dot_general(left[...], right[...], first, preferred_element_type=jnp.float32)
        product = product.astype(jnp.bfloat16)
        for block in range(per):
            at = index * per + block
            terms[at // 2, at % 2] = product[:, block * LANES : (block + 1) * LANES]

    z, high = narrow_ref[0] // 2, narrow_ref[0] % 2
    way = 1 - 2 * (wide_ref[0] % 2)
    for target, offsets in zip(targets, GROUPS):
        for index, offset in enumerate(offsets):
            chip = (z + offset * way + 2 * ring) % ring
            for half, which in enumerate((high, 1 - high)):
                send = pltpu.make_async_copy(terms.at[chip, which], target.at[index, half], out_sem.at[len(sends)])
                send.start()
                sends.append(send)

    place = owner_ref[...] * FRAME + slot_ref[...]
    chosen = (lax.broadcasted_iota(jnp.int32, (out.shape[0], x.shape[0]), 0) == place).astype(jnp.bfloat16)
    turned[:units, :] = jnp.transpose(w[:width, :])
    turned[units:, :] = jnp.transpose(w[width : 2 * width, :])
    moved = jnp.dot(chosen, pair[...], preferred_element_type=jnp.float32).astype(jnp.bfloat16)
    parts = 2
    block = out.shape[0] // parts
    for part in range(parts):
        at = pl.ds(part * block, block)
        total = jnp.dot(moved[part * block : (part + 1) * block], turned[...], preferred_element_type=jnp.float32)
        out[at, :] = total.astype(jnp.bfloat16)
        send = pltpu.make_async_copy(out.at[at], out_hbm.at[at], out_sem.at[len(sends)])
        send.start()
        sends.append(send)
    for send in sends:
        send.wait()


def table_kernel(slots_ref, out_ref):
    tokens, frames = out_ref.shape
    slots = slots_ref.shape[1]
    capacity = slots * FRAME // frames
    held = (lax.broadcasted_iota(jnp.int32, (tokens, slots), 0) == slots_ref[...]).astype(jnp.bfloat16)
    place = lax.broadcasted_iota(jnp.int32, (slots, frames), 1)
    within = lax.bitwise_and(place, FRAME - 1)
    source = lax.shift_right_logical(place, FRAME.bit_length() - 1) * capacity + within
    spread = (lax.broadcasted_iota(jnp.int32, (slots, frames), 0) == source) & (within < capacity)
    out_ref[...] = jnp.dot(held, spread.astype(jnp.bfloat16), preferred_element_type=jnp.float32).astype(jnp.bfloat16)


def combine_kernel(table_hbm, rows_hbm, out_ref, table, rows, sem):
    count = sem.shape[0] - 1
    block = rows.shape[0] // count
    first = pltpu.make_async_copy(table_hbm, table, sem.at[count])
    first.start()
    loads = []
    for index in range(count):
        at = pl.ds(index * block, block)
        loads.append(pltpu.make_async_copy(rows_hbm.at[at], rows.at[at], sem.at[index]))
        loads[-1].start()
    first.wait()
    total = jnp.zeros(out_ref.shape, jnp.float32)
    for index, load in enumerate(loads):
        load.wait()
        at = slice(index * block, (index + 1) * block)
        total += jnp.dot(table[:, at], rows[at, :], preferred_element_type=jnp.float32)
    out_ref[...] = total.astype(jnp.bfloat16)


def adam_kernel(scale, parts, shard_ref, *refs):
    weights_ref, one_ref, two_ref, out_w, out_one, out_two = refs[parts:]
    total = refs[0][...].astype(jnp.float32)
    for ref in refs[1:parts]:
        total += ref[...].astype(jnp.float32)
    gradient = jnp.transpose(total) * scale
    new_one = BETA_ONE * one_ref[0] + (1.0 - BETA_ONE) * gradient
    new_two = BETA_TWO * two_ref[0] + (1.0 - BETA_TWO) * gradient * gradient
    update = new_one / CORR_ONE / (jnp.sqrt(new_two / CORR_TWO) + EPSILON)
    kept = weights_ref[0].astype(jnp.float32) * (1.0 - LEARN_RATE * WEIGHT_DECAY)
    out_w[0] = (kept - LEARN_RATE * update).astype(jnp.bfloat16)
    out_one[0] = new_one
    out_two[0] = new_two


def ring_sum(ahead, behind, far, up_own, down_own, up_next, down_next, own, wide, narrow):
    ring = narrow // 2

    def hop(value, steps, flip=0):
        pairs = []
        for w in range(wide):
            shift = steps * (1 - 2 * (w % 2))
            for n in range(narrow):
                to = ((n // 2 + shift) % ring) * 2 + (n % 2 + flip) % 2
                pairs.append((w * narrow + n, w * narrow + to))
        return lax.ppermute(value, ("wide", "narrow"), pairs)

    def add(*values):
        total = values[0].astype(jnp.float32)
        for value in values[1:]:
            total += value.astype(jnp.float32)
        return total.astype(jnp.bfloat16)

    ahead = hop(ahead, 1)
    behind = hop(behind, -1)
    far = hop(far, 2)
    up = hop(add(far[0], ahead[0], up_own[0]), 2)
    down = hop(add(behind[0], down_own[0]), -2)
    up = hop(add(up, ahead[1], up_next[0]), 2)
    down = hop(add(down, behind[1], down_next[0]), -2)
    across = hop(add(up[1], down[1], ahead[2, 1], behind[2, 1], own[0, 1]), 0, 1)
    return (ahead, behind, own, up[None], down[None]), (across,)


def step(weights, act_rows, grad_rows, row_owner, row_slot, slot_token, moment_one, moment_two):
    wide, narrow = lax.axis_size("wide"), lax.axis_size("narrow")
    rows, width = act_rows.shape[3:]
    units = weights.shape[2]
    shard_rows = moment_one.shape[1]
    tokens = 128
    grad_scale = 1.0 / math.sqrt(rows * narrow)
    x, dy, packed = act_rows[0, 0, 0], grad_rows[0, 0, 0], weights[0]
    anywhere, vmem, smem = (pl.BlockSpec(memory_space=m) for m in (pl.ANY, pltpu.VMEM, pltpu.SMEM))
    half = jnp.bfloat16
    shard = lax.axis_index("narrow").astype(jnp.int32).reshape(1)
    column = lax.axis_index("wide").astype(jnp.int32).reshape(1)

    sizes = [len(group) for group in GROUPS]
    *blocks, outgoing = pl.pallas_call(
        expert_kernel,
        out_shape=tuple(jax.ShapeDtypeStruct((n, 2, units, shard_rows), half) for n in sizes)
        + (jax.ShapeDtypeStruct((wide * FRAME, width), half),),
        in_specs=[smem] * 2 + [vmem] * 2 + [anywhere] * 3,
        out_specs=(anywhere,) * (len(sizes) + 1),
        scratch_shapes=[
            pltpu.VMEM((rows, width), half),
            pltpu.VMEM((rows, width), half),
            pltpu.VMEM((3 * width, units), half),
            pltpu.VMEM((rows, 2 * units), half),
            pltpu.VMEM((rows, units), half),
            pltpu.VMEM((narrow // 2, 2, units, shard_rows), half),
            pltpu.VMEM((2 * units, width), half),
            pltpu.VMEM((wide * FRAME, width), half),
            pltpu.SemaphoreType.DMA((5,)),
            pltpu.SemaphoreType.DMA((2 * sum(sizes) + 2,)),
        ],
        cost_estimate=pl.CostEstimate(flops=7 * 10**9, bytes_accessed=12 * 10**6, transcendentals=3 * 10**5),
        name="expert",
    )(shard, column, row_owner[0], row_slot[0], x, dy, packed)
    stacks, parts = ring_sum(*blocks, wide, narrow)
    arrived = lax.all_to_all(
        outgoing.reshape(wide, FRAME, width), "wide", split_axis=0, concat_axis=0, tiled=True
    ).reshape(wide * FRAME, width)

    block = (1, shard_rows, units)
    whole = pl.BlockSpec(block, lambda i, s: (0, 0, 0))
    part = pl.BlockSpec((units, shard_rows), lambda i, s: (0, 0))
    stack = [pl.BlockSpec((None, None, units, shard_rows), lambda i, s, n=a.shape[0]: (n - 1, 0, 0, 0)) for a in stacks]
    new_weights, new_one, new_two = pl.pallas_call(
        lambda *refs: adam_kernel(grad_scale, len(stacks) + len(parts), *refs),
        out_shape=(
            jax.ShapeDtypeStruct(block, half),
            jax.ShapeDtypeStruct(block, jnp.float32),
            jax.ShapeDtypeStruct(block, jnp.float32),
        ),
        grid_spec=pltpu.PrefetchScalarGridSpec(
            num_scalar_prefetch=1,
            grid=(1,),
            in_specs=stack + [part] * len(parts) + [pl.BlockSpec(block, lambda i, s: (0, s[0], 0)), whole, whole],
            out_specs=(whole, whole, whole),
        ),
        compiler_params=pltpu.CompilerParams(vmem_limit_bytes=6 * 2**20),
        name="adam",
    )(shard, *stacks, *parts, weights, moment_one, moment_two)

    table = pl.pallas_call(
        table_kernel,
        out_shape=jax.ShapeDtypeStruct((tokens, wide * FRAME), half),
        in_specs=[vmem],
        out_specs=vmem,
        cost_estimate=pl.CostEstimate(flops=3 * 10**8, bytes_accessed=3 * 10**5, transcendentals=0),
        name="table",
    )(slot_token[0])
    combined = pl.pallas_call(
        combine_kernel,
        out_shape=jax.ShapeDtypeStruct((tokens, width), half),
        in_specs=[anywhere] * 2,
        out_specs=vmem,
        scratch_shapes=[
            pltpu.VMEM((tokens, wide * FRAME), half),
            pltpu.VMEM((wide * FRAME, width), half),
            pltpu.SemaphoreType.DMA((5,)),
        ],
        cost_estimate=pl.CostEstimate(flops=3 * 10**8, bytes_accessed=3 * 10**6, transcendentals=0),
        name="combine",
    )(table, arrived)
    return (combined[None, None], new_weights, new_one, new_two)


def solution(mesh):
    in_specs = (
        P("wide", None, None),
        P("wide", "narrow", None, None, None),
        P("wide", "narrow", None, None, None),
        P("wide", "narrow", None),
        P("wide", "narrow", None),
        P("wide", "narrow", None),
        P("wide", "narrow", None),
        P("wide", "narrow", None),
    )
    out_specs = (
        P("wide", "narrow", None, None),
        P("wide", "narrow", None),
        P("wide", "narrow", None),
        P("wide", "narrow", None),
    )
    return jax.shard_map(step, mesh=mesh, in_specs=in_specs, out_specs=out_specs, check_vma=False)
```

profile of v0, /device:TPU:14, one launch (start us, length us, event | category | flops | bytes accessed | tf_op | source)
XLA Modules:
  0.0 104.5 jit_solution(11500051753243124614)
XLA Ops:
  0.6 11.7 %expert.1 = (bf16[3,2,384,128]{3,2,1,0:T(8,128)(2,1)}, bf16[3,2,384,128]{3,2,1,0:T(8,128)(2,1)}, bf16[1,2,384,128]{3,2,1,0:T(8,128)(2,1)}, bf16[1,2,384,128]{3,2...) custom-call(s32[1]{0:T(128)} %bitcast.1.narrow_ref.refs_0_, ...), custom_call_target="tpu_custom_call" | custom-call | flops 7000000000 | bytes 12000000 | tf_op jit(solution)/shard_map/expert/pallas_call | solution.py:180
  12.4 0.0 copy-start.12
  12.4 0.0 copy-start.10
  12.4 8.8 %all-to-all-start = ((bf16[32,32,1024]{2,1,0:T(8,128)(2,1)}), bf16[32,32,1024]{2,1,0:T(8,128)(2,1)}, u32[]{:S(2)}, u32[]{:S(2)}) async-start(bf16[32,32,1024]{2,1,0:T(8,128)(2,1)} %bitcast.51), calls=%async_computation | async-start | bytes 4194304 | tf_op jit(solution)/shard_map/all_to_all | solution.py:202
  21.3 4.4 %collective-permute-start = (bf16[3,2,384,128]{3,2,1,0:T(8,128)(2,1)S(1)}, bf16[3,2,384,128]{3,2,1,0:T(8,128)(2,1)S(1)}, u32[]{:S(2)}, u32[]{:S(2)}) collective-permute-start(bf16[3,2,384,128]{3,2,1,0:T(8,128)(2,1)S(1)} %copy-done.11), channel_id=1, source_target_pairs={{0,2},{1,3},{2,4},{3,5},{4,6},{5,7},{6,8},{7,9},{8,10},{9,11},{10,... | collective-permute-start | bytes 1769480 | tf_op jit(solution)/shard_map/ppermute | solution.py:147
  25.7 12.2 %collective-permute-start.1 = (bf16[3,2,384,128]{3,2,1,0:T(8,128)(2,1)}, bf16[3,2,384,128]{3,2,1,0:T(8,128)(2,1)S(1)}, u32[]{:S(2)}, u32[]{:S(2)}) collective-permute-start(bf16[3,2,384,128]{3,2,1,0:T(8,128)(2,1)} %get-tuple-element.18), channel_id=1, source_target_pairs={{0,22},{1,23},{2,0},{3,1},{4,2},{5,3},{6,4},{7,5},{8,6},{9,7},{10,... | collective-permute-start | bytes 1769480 | tf_op jit(solution)/shard_map/ppermute | solution.py:147
  38.0 1.9 %collective-permute-start.2 = (bf16[1,2,384,128]{3,2,1,0:T(8,128)(2,1)S(1)}, bf16[1,2,384,128]{3,2,1,0:T(8,128)(2,1)S(1)}, u32[]{:S(2)}, u32[]{:S(2)}) collective-permute-start(bf16[1,2,384,128]{3,2,1,0:T(8,128)(2,1)S(1)} %copy-done.12), channel_id=1, source_target_pairs={{0,4},{1,5},{2,6},{3,7},{4,8},{5,9},{6,10},{7,11},{8,12},{9,13},{1... | collective-permute-start | bytes 589832 | tf_op jit(solution)/shard_map/ppermute | solution.py:147
  39.9 16.0 %collective-permute-done.2 = bf16[1,2,384,128]{3,2,1,0:T(8,128)(2,1)S(1)} collective-permute-done((bf16[1,2,384,128]{3,2,1,0:T(8,128)(2,1)S(1)}, bf16[1,2,384,128]{3,2,1,0:T(8,128)(2,1)S(1)}, u32[]{:S(2)}, u32[]{:S(2)}) %collective-permute-start.2) | collective-permute-done | bytes 196640 | tf_op jit(solution)/shard_map/ppermute | solution.py:147
  55.9 0.0 collective-permute-done.refs_1_
  55.9 0.1 fusion.2
  55.9 0.0 copy-start
  56.0 2.1 %collective-permute-start.3 = (bf16[2,384,128]{2,1,0:T(8,128)(2,1)S(1)}, bf16[2,384,128]{2,1,0:T(8,128)(2,1)S(1)}, u32[]{:S(2)}, u32[]{:S(2)}) collective-permute-start(bf16[2,384,128]{2,1,0:T(8,128)(2,1)S(1)} %fusion.2), channel_id=1, source_target_pairs={{0,4},{1,5},{2,6},{3,7},{4,8},{5,9},{6,10},{7,11},{8,12},{9,13},{1... | collective-permute-start | bytes 589832 | tf_op jit(solution)/shard_map/ppermute | solution.py:147
  58.0 0.0 collective-permute-done.1.refs_2_
  58.0 1.0 fusion.3
  59.0 6.0 %collective-permute-start.5 = (bf16[2,384,128]{2,1,0:T(8,128)(2,1)S(1)}, bf16[2,384,128]{2,1,0:T(8,128)(2,1)S(1)}, u32[]{:S(2)}, u32[]{:S(2)}) collective-permute-start(bf16[2,384,128]{2,1,0:T(8,128)(2,1)S(1)} %fusion.3), channel_id=1, source_target_pairs={{0,20},{1,21},{2,22},{3,23},{4,0},{5,1},{6,2},{7,3},{8,4},{9,5},{1... | collective-permute-start | bytes 589832 | tf_op jit(solution)/shard_map/ppermute | solution.py:147
  65.1 4.9 %collective-permute-done.3 = bf16[2,384,128]{2,1,0:T(8,128)(2,1)S(1)} collective-permute-done((bf16[2,384,128]{2,1,0:T(8,128)(2,1)S(1)}, bf16[2,384,128]{2,1,0:T(8,128)(2,1)S(1)}, u32[]{:S(2)}, u32[]{:S(2)}) %collective-permute-start.3) | collective-permute-done | bytes 196640 | tf_op jit(solution)/shard_map/ppermute | solution.py:147
  69.9 1.0 fusion.1
  70.9 2.7 %collective-permute-start.4 = (bf16[2,384,128]{2,1,0:T(8,128)(2,1)S(1)}, bf16[2,384,128]{2,1,0:T(8,128)(2,1)S(1)}, u32[]{:S(2)}, u32[]{:S(2)}) collective-permute-start(bf16[2,384,128]{2,1,0:T(8,128)(2,1)S(1)} %fusion.1), channel_id=1, source_target_pairs={{0,4},{1,5},{2,6},{3,7},{4,8},{5,9},{6,10},{7,11},{8,12},{9,13},{1... | collective-permute-start | bytes 589832 | tf_op jit(solution)/shard_map/ppermute | solution.py:147
  73.7 0.1 fusion
  73.8 5.2 %collective-permute-start.6 = (bf16[2,384,128]{2,1,0:T(8,128)(2,1)S(1)}, bf16[2,384,128]{2,1,0:T(8,128)(2,1)S(1)}, u32[]{:S(2)}, u32[]{:S(2)}) collective-permute-start(bf16[2,384,128]{2,1,0:T(8,128)(2,1)S(1)} %fusion), channel_id=1, source_target_pairs={{0,20},{1,21},{2,22},{3,23},{4,0},{5,1},{6,2},{7,3},{8,4},{9,5},{1... | collective-permute-start | bytes 589832 | tf_op jit(solution)/shard_map/ppermute | solution.py:147
  79.0 7.3 %collective-permute-done.4 = bf16[2,384,128]{2,1,0:T(8,128)(2,1)S(1)} collective-permute-done((bf16[2,384,128]{2,1,0:T(8,128)(2,1)S(1)}, bf16[2,384,128]{2,1,0:T(8,128)(2,1)S(1)}, u32[]{:S(2)}, u32[]{:S(2)}) %collective-permute-start.4) | collective-permute-done | bytes 196640 | tf_op jit(solution)/shard_map/ppermute | solution.py:147
  86.3 0.8 fusion.4
  87.1 2.4 %collective-permute-start.7 = (bf16[384,128]{1,0:T(8,128)(2,1)}, bf16[384,128]{1,0:T(8,128)(2,1)}, u32[]{:S(2)}, u32[]{:S(2)}) collective-permute-start(bf16[384,128]{1,0:T(8,128)(2,1)} %fusion.4), channel_id=1, source_target_pairs={{0,1},{1,0},{2,3},{3,2},{4,5},{5,4},{6,7},{7,6},{8,9},{9,8},{10,11... | collective-permute-start | bytes 294920 | tf_op jit(solution)/shard_map/ppermute | solution.py:147
  89.5 1.9 %table.1.table_hbm = bf16[128,1024]{1,0:T(8,128)(2,1)} custom-call(s32[1,960]{1,0:T(1,128)} %bitcast.55), custom_call_target="tpu_custom_call" | custom-call | flops 300000000 | bytes 300000 | tf_op jit(solution)/shard_map/table/pallas_call | solution.py:227
  91.4 4.0 %collective-permute-done.7.refs_6_ = bf16[384,128]{1,0:T(8,128)(2,1)} collective-permute-done((bf16[384,128]{1,0:T(8,128)(2,1)}, bf16[384,128]{1,0:T(8,128)(2,1)}, u32[]{:S(2)}, u32[]{:S(2)}) %collective-permute-start.7) | collective-permute-done | bytes 98336 | tf_op jit(solution)/shard_map/ppermute | solution.py:147
  95.4 0.9 copy-done.2
  96.3 0.9 copy-done.4
  97.3 0.9 copy-done.6
  98.2 0.9 copy-done.7
  99.1 0.9 copy-done.8
  100.1 1.9 %adam.1 = (bf16[1,128,384]{2,1,0:T(8,128)(2,1)}, f32[1,128,384]{2,1,0:T(8,128)}, f32[1,128,384]{2,1,0:T(8,128)}) custom-call(s32[1]{0:T(128)} %bitcast.1.narrow_ref.refs_0_, bf16[3,2,384,128]{3,2,1,0:T(8,128)(2,1)S(1)} %collective-permute-done.refs_1_, bf16[3,2,384,128]{3,2,1,0:T(8,128)(2,1)S(1)} %collective-permute-done.1.refs_2_, ...), custom_call_target="tpu_custom_call" | custom-call | tf_op jit(solution)/shard_map/adam/pallas_call | solution.py:210
  102.0 2.6 %combine.1 = bf16[128,1024]{1,0:T(8,128)(2,1)} custom-call(bf16[128,1024]{1,0:T(8,128)(2,1)} %table.1.table_hbm, bf16[1024,1024]{1,0:T(8,128)(2,1)} %bitcast.9.rows_hbm), custom_call_target="tpu_custom_call" | custom-call | flops 300000000 | bytes 3000000 | tf_op jit(solution)/shard_map/combine/pallas_call | solution.py:235
  (21 shorter events, 0.0 us)
Async XLA Ops:
  12.4 8.9 %copy-start.11 = (bf16[3,2,384,128]{3,2,1,0:T(8,128)(2,1)S(1)}, bf16[3,2,384,128]{3,2,1,0:T(8,128)(2,1)}, u32[]{:S(2)}) copy-start(bf16[3,2,384,128]{3,2,1,0:T(8,128)(2,1)} %get-tuple-element.17) | copy-start | bytes 1769476
  12.4 25.5 %copy-start.12 = (bf16[1,2,384,128]{3,2,1,0:T(8,128)(2,1)S(1)}, bf16[1,2,384,128]{3,2,1,0:T(8,128)(2,1)}, u32[]{:S(2)}) copy-start(bf16[1,2,384,128]{3,2,1,0:T(8,128)(2,1)} %get-tuple-element.20) | copy-start | bytes 589828
  12.4 43.4 %copy-start.10 = (bf16[1,2,384,128]{3,2,1,0:T(8,128)(2,1)S(1)}, bf16[1,2,384,128]{3,2,1,0:T(8,128)(2,1)}, u32[]{:S(2)}) copy-start(bf16[1,2,384,128]{3,2,1,0:T(8,128)(2,1)} %get-tuple-element.21) | copy-start | bytes 589828
  12.4 89.5 %all-to-all-start = ((bf16[32,32,1024]{2,1,0:T(8,128)(2,1)}), bf16[32,32,1024]{2,1,0:T(8,128)(2,1)}, u32[]{:S(2)}, u32[]{:S(2)}) async-start(bf16[32,32,1024]{2,1,0:T(8,128)(2,1)} %bitcast.51), calls=%async_computation | async-start | bytes 4194304 | tf_op jit(solution)/shard_map/all_to_all | solution.py:202
  21.3 52.4 %copy-start.9 = (bf16[1,2,384,128]{3,2,1,0:T(8,128)(2,1)S(1)}, bf16[1,2,384,128]{3,2,1,0:T(8,128)(2,1)}, u32[]{:S(2)}) copy-start(bf16[1,2,384,128]{3,2,1,0:T(8,128)(2,1)} %get-tuple-element.24) | copy-start | bytes 589828
  21.3 65.1 %copy-start.1 = (bf16[1,2,384,128]{3,2,1,0:T(8,128)(2,1)S(1)}, bf16[1,2,384,128]{3,2,1,0:T(8,128)(2,1)}, u32[]{:S(2)}) copy-start(bf16[1,2,384,128]{3,2,1,0:T(8,128)(2,1)} %get-tuple-element.19.refs_3_) | copy-start | bytes 589828
  21.3 34.6 %collective-permute-start = (bf16[3,2,384,128]{3,2,1,0:T(8,128)(2,1)S(1)}, bf16[3,2,384,128]{3,2,1,0:T(8,128)(2,1)S(1)}, u32[]{:S(2)}, u32[]{:S(2)}) collective-permute-start(bf16[3,2,384,128]{3,2,1,0:T(8,128)(2,1)S(1)} %copy-done.11), channel_id=1, source_target_pairs={{0,2},{1,3},{2,4},{3,5},{4,6},{5,7},{6,8},{7,9},{8,10},{9,11},{10,... | collective-permute-start | bytes 1769480 | tf_op jit(solution)/shard_map/ppermute | solution.py:147
  25.7 32.3 %collective-permute-start.1 = (bf16[3,2,384,128]{3,2,1,0:T(8,128)(2,1)}, bf16[3,2,384,128]{3,2,1,0:T(8,128)(2,1)S(1)}, u32[]{:S(2)}, u32[]{:S(2)}) collective-permute-start(bf16[3,2,384,128]{3,2,1,0:T(8,128)(2,1)} %get-tuple-element.18), channel_id=1, source_target_pairs={{0,22},{1,23},{2,0},{3,1},{4,2},{5,3},{6,4},{7,5},{8,6},{9,7},{10,... | collective-permute-start | bytes 1769480 | tf_op jit(solution)/shard_map/ppermute | solution.py:147
  38.0 17.9 %collective-permute-start.2 = (bf16[1,2,384,128]{3,2,1,0:T(8,128)(2,1)S(1)}, bf16[1,2,384,128]{3,2,1,0:T(8,128)(2,1)S(1)}, u32[]{:S(2)}, u32[]{:S(2)}) collective-permute-start(bf16[1,2,384,128]{3,2,1,0:T(8,128)(2,1)S(1)} %copy-done.12), channel_id=1, source_target_pairs={{0,4},{1,5},{2,6},{3,7},{4,8},{5,9},{6,10},{7,11},{8,12},{9,13},{1... | collective-permute-start | bytes 589832 | tf_op jit(solution)/shard_map/ppermute | solution.py:147
  55.9 39.5 %copy-start = (bf16[1,3072,384]{2,1,0:T(8,128)(2,1)S(1)}, bf16[1,3072,384]{2,1,0:T(8,128)(2,1)}, u32[]{:S(2)}) copy-start(bf16[1,3072,384]{2,1,0:T(8,128)(2,1)} %refs_7_.1) | copy-start | bytes 7077892
  56.0 14.0 %collective-permute-start.3 = (bf16[2,384,128]{2,1,0:T(8,128)(2,1)S(1)}, bf16[2,384,128]{2,1,0:T(8,128)(2,1)S(1)}, u32[]{:S(2)}, u32[]{:S(2)}) collective-permute-start(bf16[2,384,128]{2,1,0:T(8,128)(2,1)S(1)} %fusion.2), channel_id=1, source_target_pairs={{0,4},{1,5},{2,6},{3,7},{4,8},{5,9},{6,10},{7,11},{8,12},{9,13},{1... | collective-permute-start | bytes 589832 | tf_op jit(solution)/shard_map/ppermute | solution.py:147
  59.0 14.7 %collective-permute-start.5 = (bf16[2,384,128]{2,1,0:T(8,128)(2,1)S(1)}, bf16[2,384,128]{2,1,0:T(8,128)(2,1)S(1)}, u32[]{:S(2)}, u32[]{:S(2)}) collective-permute-start(bf16[2,384,128]{2,1,0:T(8,128)(2,1)S(1)} %fusion.3), channel_id=1, source_target_pairs={{0,20},{1,21},{2,22},{3,23},{4,0},{5,1},{6,2},{7,3},{8,4},{9,5},{1... | collective-permute-start | bytes 589832 | tf_op jit(solution)/shard_map/ppermute | solution.py:147
  70.9 15.4 %collective-permute-start.4 = (bf16[2,384,128]{2,1,0:T(8,128)(2,1)S(1)}, bf16[2,384,128]{2,1,0:T(8,128)(2,1)S(1)}, u32[]{:S(2)}, u32[]{:S(2)}) collective-permute-start(bf16[2,384,128]{2,1,0:T(8,128)(2,1)S(1)} %fusion.1), channel_id=1, source_target_pairs={{0,4},{1,5},{2,6},{3,7},{4,8},{5,9},{6,10},{7,11},{8,12},{9,13},{1... | collective-permute-start | bytes 589832 | tf_op jit(solution)/shard_map/ppermute | solution.py:147
  73.8 12.5 %collective-permute-start.6 = (bf16[2,384,128]{2,1,0:T(8,128)(2,1)S(1)}, bf16[2,384,128]{2,1,0:T(8,128)(2,1)S(1)}, u32[]{:S(2)}, u32[]{:S(2)}) collective-permute-start(bf16[2,384,128]{2,1,0:T(8,128)(2,1)S(1)} %fusion), channel_id=1, source_target_pairs={{0,20},{1,21},{2,22},{3,23},{4,0},{5,1},{6,2},{7,3},{8,4},{9,5},{1... | collective-permute-start | bytes 589832 | tf_op jit(solution)/shard_map/ppermute | solution.py:147
  86.3 0.8 copy-start.3
  86.3 3.1 %copy-start.5 = (bf16[2,384,128]{2,1,0:T(8,128)(2,1)}, bf16[2,384,128]{2,1,0:T(8,128)(2,1)S(1)}, u32[]{:S(2)}) copy-start(bf16[2,384,128]{2,1,0:T(8,128)(2,1)S(1)} %collective-permute-done.6) | copy-start | bytes 589828
  87.1 8.3 %collective-permute-start.7 = (bf16[384,128]{1,0:T(8,128)(2,1)}, bf16[384,128]{1,0:T(8,128)(2,1)}, u32[]{:S(2)}, u32[]{:S(2)}) collective-permute-start(bf16[384,128]{1,0:T(8,128)(2,1)} %fusion.4), channel_id=1, source_target_pairs={{0,1},{1,0},{2,3},{3,2},{4,5},{5,4},{6,7},{7,6},{8,9},{9,8},{10,11... | collective-permute-start | bytes 294920 | tf_op jit(solution)/shard_map/ppermute | solution.py:147
  95.4 0.9 copy-start.2
  96.3 0.9 copy-start.4
  97.3 0.9 copy-start.6
  98.2 0.9 copy-start.7
  99.1 0.9 copy-start.8
where the time goes:
time: 105 us
  starting transfers between devices  45.8 us (44%)
  waiting for transfers between devices  32.2 us (31%)
  Pallas kernels  18.1 us (17%)
  local copies, waits for them, and re-layouts  4.67 us (4%)
  other arithmetic  2.91 us (3%)
    ppermute x8, starting transfers between devices, hop(): return lax.ppermute(value, ('wide', 'narrow'), pairs)  37 us
    ppermute x8, waiting for transfers between devices, hop(): return lax.ppermute(value, ('wide', 'narrow'), pairs)  32.2 us
    pallas_call x1, Pallas kernels, step(): pl.pallas_call(expert_kernel, out_shape=tuple((jax.ShapeDtypeStruct((n, 2...  11.7 us
    all_to_all x1, starting transfers between devices, step(): lax.all_to_all(outgoing.reshape(wide, FRAME, width), 'wide', split_axis=0...  8.82 us
    unnamed x26, local copies, waits for them, and re-layouts  4.67 us
    convert_element_type x5, other arithmetic, add(): return total.astype(jnp.bfloat16)  2.91 us
    pallas_call x1, Pallas kernels, step(): pl.pallas_call(combine_kernel, out_shape=jax.ShapeDtypeStruct((tokens, wi...  2.59 us
  transfers between devices with their start and end apart: 9, of which 4 were waited for; matrix products, arithmetic and copies ran while one was open for 3% of the time, Pallas kernels for 4%

commit v1 on v0

--- a/solution.py
+++ b/solution.py
@@ -24,41 +24,44 @@
 
 def expert_kernel(narrow_ref, wide_ref, owner_ref, slot_ref, x_hbm, dy_hbm, w_hbm, *refs):
     targets, out_hbm = refs[: len(GROUPS)], refs[len(GROUPS)]
-    x, dy, w, pair, hidden, terms, turned, out, in_sem, out_sem = refs[len(GROUPS) + 1 :]
-    width, units = x.shape[1], w.shape[1]
+    x, dy, w, w_down, pair, hidden, terms, turned, out, in_sem, out_sem = refs[len(GROUPS) + 1 :]
+    width, units = x.shape[1], hidden.shape[1]
     loads = [
         pltpu.make_async_copy(x_hbm, x, in_sem.at[0]),
-        pltpu.make_async_copy(w_hbm.at[pl.ds(0, width)], w.at[pl.ds(0, width)], in_sem.at[1]),
-        pltpu.make_async_copy(w_hbm.at[pl.ds(width, width)], w.at[pl.ds(width, width)], in_sem.at[2]),
+        pltpu.make_async_copy(w_hbm.at[pl.ds(0, width)], w.at[:, pl.ds(0, units)], in_sem.at[1]),
+        pltpu.make_async_copy(w_hbm.at[pl.ds(width, width)], w.at[:, pl.ds(units, units)], in_sem.at[2]),
         pltpu.make_async_copy(dy_hbm, dy, in_sem.at[3]),
-        pltpu.make_async_copy(w_hbm.at[pl.ds(2 * width, width)], w.at[pl.ds(2 * width, width)], in_sem.at[4]),
+        pltpu.make_async_copy(w_hbm.at[pl.ds(2 * width, width)], w_down, in_sem.at[4]),
     ]
     for load in loads:
         load.start()
-    loads[0].wait()
-    loads[1].wait()
-    gate = jnp.dot(x[...], w[:width, :], preferred_element_type=jnp.float32)
-    loads[2].wait()
-    up = jnp.dot(x[...], w[width : 2 * width, :], preferred_element_type=jnp.float32)
-    loads[3].wait()
-    loads[4].wait()
-    d_hidden = jnp.dot(dy[...], w[2 * width :, :], preferred_element_type=jnp.float32)
-    prob = jax.nn.sigmoid(gate)
-    active = gate * prob
-    hidden[...] = (active * up).astype(jnp.bfloat16)
-    pair[:, units:] = (d_hidden * active).astype(jnp.bfloat16)
-    pair[:, :units] = (d_hidden * up * prob * (1.0 + gate * (1.0 - prob))).astype(jnp.bfloat16)
+    for load in loads[:3]:
+        load.wait()
+    rows = x.shape[0]
+    cut = -(-rows // 32) * 16
+    blocks = (slice(0, cut), slice(cut, rows))
+    products = [jnp.dot(x[at, :], w[...], preferred_element_type=jnp.float32) for at in blocks]
+    for load in loads[3:]:
+        load.wait()
+    for at, both in zip(blocks, products):
+        gate, up = both[:, :units], both[:, units:]
+        d_hidden = jnp.dot(dy[at, :], w_down[...], preferred_element_type=jnp.float32)
+        prob = jax.nn.sigmoid(gate)
+        active = gate * prob
+        hidden[at, :] = (active * up).astype(jnp.bfloat16)
+        pair[at, units:] = (d_hidden * active).astype(jnp.bfloat16)
+        pair[at, :units] = (d_hidden * up * prob * (1.0 + gate * (1.0 - prob))).astype(jnp.bfloat16)
     sends = []
 
     ring = terms.shape[0]
     per = width // LANES
     first = (((0,), (0,)), ((), ()))
-    for index, (left, right) in enumerate(((pair.at[:, :units], x), (pair.at[:, units:], x), (hidden, dy))):
+    for start, left, right in ((0, pair, x), (2 * per, hidden, dy)):
         product = lax.dot_general(left[...], right[...], first, preferred_element_type=jnp.float32)
         product = product.astype(jnp.bfloat16)
-        for block in range(per):
-            at = index * per + block
-            terms[at // 2, at % 2] = product[:, block * LANES : (block + 1) * LANES]
+        for at in range(start, start + per * left.shape[1] // units):
+            row, block = (at - start) // per * units, at % per * LANES
+            terms[at // 2, at % 2] = product[row : row + units, block : block + LANES]
 
     z, high = narrow_ref[0] // 2, narrow_ref[0] % 2
     way = 1 - 2 * (wide_ref[0] % 2)
@@ -72,8 +75,7 @@
 
     place = owner_ref[...] * FRAME + slot_ref[...]
     chosen = (lax.broadcasted_iota(jnp.int32, (out.shape[0], x.shape[0]), 0) == place).astype(jnp.bfloat16)
-    turned[:units, :] = jnp.transpose(w[:width, :])
-    turned[units:, :] = jnp.transpose(w[width : 2 * width, :])
+    turned[...] = jnp.transpose(w[...])
     moved = jnp.dot(chosen, pair[...], preferred_element_type=jnp.float32).astype(jnp.bfloat16)
     parts = 2
     block = out.shape[0] // parts
@@ -100,23 +102,8 @@
     out_ref[...] = jnp.dot(held, spread.astype(jnp.bfloat16), preferred_element_type=jnp.float32).astype(jnp.bfloat16)
 
 
-def combine_kernel(table_hbm, rows_hbm, out_ref, table, rows, sem):
-    count = sem.shape[0] - 1
-    block = rows.shape[0] // count
-    first = pltpu.make_async_copy(table_hbm, table, sem.at[count])
-    first.start()
-    loads = []
-    for index in range(count):
-        at = pl.ds(index * block, block)
-        loads.append(pltpu.make_async_copy(rows_hbm.at[at], rows.at[at], sem.at[index]))
-        loads[-1].start()
-    first.wait()
-    total = jnp.zeros(out_ref.shape, jnp.float32)
-    for index, load in enumerate(loads):
-        load.wait()
-        at = slice(index * block, (index + 1) * block)
-        total += jnp.dot(table[:, at], rows[at, :], preferred_element_type=jnp.float32)
-    out_ref[...] = total.astype(jnp.bfloat16)
+def combine_kernel(table_ref, rows_ref, out_ref):
+    out_ref[...] = jnp.dot(table_ref[...], rows_ref[...], preferred_element_type=jnp.float32).astype(jnp.bfloat16)
 
 
 def adam_kernel(scale, parts, shard_ref, *refs):
@@ -186,7 +173,8 @@
         scratch_shapes=[
             pltpu.VMEM((rows, width), half),
             pltpu.VMEM((rows, width), half),
-            pltpu.VMEM((3 * width, units), half),
+            pltpu.VMEM((width, 2 * units), half),
+            pltpu.VMEM((width, units), half),
             pltpu.VMEM((rows, 2 * units), half),
             pltpu.VMEM((rows, units), half),
             pltpu.VMEM((narrow // 2, 2, units, shard_rows), half),
@@ -229,19 +217,16 @@
         out_shape=jax.ShapeDtypeStruct((tokens, wide * FRAME), half),
         in_specs=[vmem],
         out_specs=vmem,
-        cost_estimate=pl.CostEstimate(flops=3 * 10**8, bytes_accessed=3 * 10**5, transcendentals=0),
+        compiler_params=pltpu.CompilerParams(vmem_limit_bytes=16 * 2**20),
+        cost_estimate=pl.CostEstimate(flops=4 * 10**9, bytes_accessed=3 * 10**5, transcendentals=0),
         name="table",
     )(slot_token[0])
     combined = pl.pallas_call(
         combine_kernel,
         out_shape=jax.ShapeDtypeStruct((tokens, width), half),
-        in_specs=[anywhere] * 2,
+        in_specs=[vmem] * 2,
         out_specs=vmem,
-        scratch_shapes=[
-            pltpu.VMEM((tokens, wide * FRAME), half),
-            pltpu.VMEM((wide * FRAME, width), half),
-            pltpu.SemaphoreType.DMA((5,)),
-        ],
+        compiler_params=pltpu.CompilerParams(vmem_limit_bytes=16 * 2**20),
         cost_estimate=pl.CostEstimate(flops=3 * 10**8, bytes_accessed=3 * 10**6, transcendentals=0),
         name="combine",
     )(table, arrived)

time: 105 us -> 95.2 us (0.907)
  the two profiles are of different devices: /device:TPU:14 before, /device:TPU:8 now
where the time goes in v1:
time: 95.2 us; the launch traced here: 94.7 us
  starting transfers between devices  47.8 us (50%)
  waiting for transfers between devices  31.6 us (33%)
  Pallas kernels  14 us (15%)
    ppermute x8, starting transfers between devices, hop(): return lax.ppermute(value, ('wide', 'narrow'), pairs)  34.6 us
    ppermute x8, waiting for transfers between devices, hop(): return lax.ppermute(value, ('wide', 'narrow'), pairs)  31.6 us
    all_to_all x1, starting transfers between devices, step(): lax.all_to_all(outgoing.reshape(wide, FRAME, width), 'wide', split_axis=0...  13.3 us
    pallas_call x1, Pallas kernels, step(): pl.pallas_call(expert_kernel, out_shape=tuple((jax.ShapeDtypeStruct((n, 2...  11.3 us
  transfers between devices with their start and end apart: 9, of which 4 were waited for; matrix products, arithmetic and copies ran while one was open for 0% of the time, Pallas kernels for 2%

profile of v1, /device:TPU:8, one launch (start us, length us, event | category | flops | bytes accessed | tf_op | source)
XLA Modules:
  0.0 94.7 jit_solution(8778718654674830190)
XLA Ops:
  0.6 11.3 %expert.1 = (bf16[3,2,384,128]{3,2,1,0:T(8,128)(2,1)}, bf16[3,2,384,128]{3,2,1,0:T(8,128)(2,1)}, bf16[1,2,384,128]{3,2,1,0:T(8,128)(2,1)}, bf16[1,2,384,128]{3,2...) custom-call(s32[1]{0:T(128)} %bitcast.1.narrow_ref.refs_0_, ...), custom_call_target="tpu_custom_call" | custom-call | flops 7000000000 | bytes 12000000 | tf_op jit(solution)/shard_map/expert/pallas_call | solution.py:167
  12.0 0.0 copy-start.8
  12.0 0.0 copy-start.7
  12.0 13.3 %all-to-all-start = ((bf16[32,32,1024]{2,1,0:T(8,128)(2,1)}), bf16[32,32,1024]{2,1,0:T(8,128)(2,1)S(1)}, u32[]{:S(2)}, u32[]{:S(2)}) async-start(bf16[32,32,1024]{2,1,0:T(8,128)(2,1)} %bitcast.53), calls=%async_computation | async-start | bytes 4194304 | tf_op jit(solution)/shard_map/all_to_all | solution.py:190
  25.3 0.0 copy-start.4
  25.3 2.1 %collective-permute-start = (bf16[3,2,384,128]{3,2,1,0:T(8,128)(2,1)}, bf16[3,2,384,128]{3,2,1,0:T(8,128)(2,1)S(1)}, u32[]{:S(2)}, u32[]{:S(2)}) collective-permute-start(bf16[3,2,384,128]{3,2,1,0:T(8,128)(2,1)} %get-tuple-element.17), channel_id=1, source_target_pairs={{0,2},{1,3},{2,4},{3,5},{4,6},{5,7},{6,8},{7,9},{8,10},{9,11},{10,... | collective-permute-start | bytes 1769480 | tf_op jit(solution)/shard_map/ppermute | solution.py:134
  27.4 10.1 %collective-permute-start.1 = (bf16[3,2,384,128]{3,2,1,0:T(8,128)(2,1)}, bf16[3,2,384,128]{3,2,1,0:T(8,128)(2,1)S(1)}, u32[]{:S(2)}, u32[]{:S(2)}) collective-permute-start(bf16[3,2,384,128]{3,2,1,0:T(8,128)(2,1)} %get-tuple-element.18), channel_id=1, source_target_pairs={{0,22},{1,23},{2,0},{3,1},{4,2},{5,3},{6,4},{7,5},{8,6},{9,7},{10,... | collective-permute-start | bytes 1769480 | tf_op jit(solution)/shard_map/ppermute | solution.py:134
  37.5 1.9 %collective-permute-start.2 = (bf16[1,2,384,128]{3,2,1,0:T(8,128)(2,1)}, bf16[1,2,384,128]{3,2,1,0:T(8,128)(2,1)S(1)}, u32[]{:S(2)}, u32[]{:S(2)}) collective-permute-start(bf16[1,2,384,128]{3,2,1,0:T(8,128)(2,1)} %get-tuple-element.20), channel_id=1, source_target_pairs={{0,4},{1,5},{2,6},{3,7},{4,8},{5,9},{6,10},{7,11},{8,12},{9,13},{1... | collective-permute-start | bytes 589832 | tf_op jit(solution)/shard_map/ppermute | solution.py:134
  39.4 16.2 %collective-permute-done.2 = bf16[1,2,384,128]{3,2,1,0:T(8,128)(2,1)S(1)} collective-permute-done((bf16[1,2,384,128]{3,2,1,0:T(8,128)(2,1)}, bf16[1,2,384,128]{3,2,1,0:T(8,128)(2,1)S(1)}, u32[]{:S(2)}, u32[]{:S(2)}) %collective-permute-start.2) | collective-permute-done | bytes 196640 | tf_op jit(solution)/shard_map/ppermute | solution.py:134
  55.6 0.0 collective-permute-done.refs_1_
  55.6 0.1 fusion.2
  55.7 1.9 %collective-permute-start.3 = (bf16[2,384,128]{2,1,0:T(8,128)(2,1)S(1)}, bf16[2,384,128]{2,1,0:T(8,128)(2,1)S(1)}, u32[]{:S(2)}, u32[]{:S(2)}) collective-permute-start(bf16[2,384,128]{2,1,0:T(8,128)(2,1)S(1)} %fusion.2), channel_id=1, source_target_pairs={{0,4},{1,5},{2,6},{3,7},{4,8},{5,9},{6,10},{7,11},{8,12},{9,13},{1... | collective-permute-start | bytes 589832 | tf_op jit(solution)/shard_map/ppermute | solution.py:134
  57.6 0.0 collective-permute-done.1.refs_2_
  57.6 0.1 fusion.3
  57.7 6.0 %collective-permute-start.5 = (bf16[2,384,128]{2,1,0:T(8,128)(2,1)S(1)}, bf16[2,384,128]{2,1,0:T(8,128)(2,1)S(1)}, u32[]{:S(2)}, u32[]{:S(2)}) collective-permute-start(bf16[2,384,128]{2,1,0:T(8,128)(2,1)S(1)} %fusion.3), channel_id=1, source_target_pairs={{0,20},{1,21},{2,22},{3,23},{4,0},{5,1},{6,2},{7,3},{8,4},{9,5},{1... | collective-permute-start | bytes 589832 | tf_op jit(solution)/shard_map/ppermute | solution.py:134
  63.8 5.7 %collective-permute-done.3 = bf16[2,384,128]{2,1,0:T(8,128)(2,1)S(1)} collective-permute-done((bf16[2,384,128]{2,1,0:T(8,128)(2,1)S(1)}, bf16[2,384,128]{2,1,0:T(8,128)(2,1)S(1)}, u32[]{:S(2)}, u32[]{:S(2)}) %collective-permute-start.3) | collective-permute-done | bytes 196640 | tf_op jit(solution)/shard_map/ppermute | solution.py:134
  69.5 0.1 fusion.1
  69.6 2.9 %collective-permute-start.4 = (bf16[2,384,128]{2,1,0:T(8,128)(2,1)S(1)}, bf16[2,384,128]{2,1,0:T(8,128)(2,1)S(1)}, u32[]{:S(2)}, u32[]{:S(2)}) collective-permute-start(bf16[2,384,128]{2,1,0:T(8,128)(2,1)S(1)} %fusion.1), channel_id=1, source_target_pairs={{0,4},{1,5},{2,6},{3,7},{4,8},{5,9},{6,10},{7,11},{8,12},{9,13},{1... | collective-permute-start | bytes 589832 | tf_op jit(solution)/shard_map/ppermute | solution.py:134
  72.5 0.0 collective-permute-done.5
  72.5 0.1 fusion
  72.6 5.0 %collective-permute-start.6 = (bf16[2,384,128]{2,1,0:T(8,128)(2,1)S(1)}, bf16[2,384,128]{2,1,0:T(8,128)(2,1)S(1)}, u32[]{:S(2)}, u32[]{:S(2)}) collective-permute-start(bf16[2,384,128]{2,1,0:T(8,128)(2,1)S(1)} %fusion), channel_id=1, source_target_pairs={{0,20},{1,21},{2,22},{3,23},{4,0},{5,1},{6,2},{7,3},{8,4},{9,5},{1... | collective-permute-start | bytes 589832 | tf_op jit(solution)/shard_map/ppermute | solution.py:134
  77.6 6.8 %collective-permute-done.4 = bf16[2,384,128]{2,1,0:T(8,128)(2,1)S(1)} collective-permute-done((bf16[2,384,128]{2,1,0:T(8,128)(2,1)S(1)}, bf16[2,384,128]{2,1,0:T(8,128)(2,1)S(1)}, u32[]{:S(2)}, u32[]{:S(2)}) %collective-permute-start.4) | collective-permute-done | bytes 196640 | tf_op jit(solution)/shard_map/ppermute | solution.py:134
  84.4 0.0 collective-permute-done.6
  84.4 0.1 fusion.4
  84.5 4.6 %collective-permute-start.7 = (bf16[384,128]{1,0:T(8,128)(2,1)S(1)}, bf16[384,128]{1,0:T(8,128)(2,1)S(1)}, u32[]{:S(2)}, u32[]{:S(2)}) collective-permute-start(bf16[384,128]{1,0:T(8,128)(2,1)S(1)} %fusion.4), channel_id=1, source_target_pairs={{0,1},{1,0},{2,3},{3,2},{4,5},{5,4},{6,7},{7,6},{8,9},{9,8},{10,11... | collective-permute-start | bytes 294920 | tf_op jit(solution)/shard_map/ppermute | solution.py:134
  89.1 0.0 copy-start
  89.1 0.0 copy-start.2
  89.1 0.0 copy-start.3
  89.1 0.5 table.1.table_ref
  89.7 2.9 %collective-permute-done.7.refs_6_ = bf16[384,128]{1,0:T(8,128)(2,1)S(1)} collective-permute-done((bf16[384,128]{1,0:T(8,128)(2,1)S(1)}, bf16[384,128]{1,0:T(8,128)(2,1)S(1)}, u32[]{:S(2)}, u32[]{:S(2)}) %collective-permute-start.7) | collective-permute-done | bytes 98336 | tf_op jit(solution)/shard_map/ppermute | solution.py:134
  92.5 1.0 %adam.1 = (bf16[1,128,384]{2,1,0:T(8,128)(2,1)}, f32[1,128,384]{2,1,0:T(8,128)}, f32[1,128,384]{2,1,0:T(8,128)}) custom-call(s32[1]{0:T(128)} %bitcast.1.narrow_ref.refs_0_, bf16[3,2,384,128]{3,2,1,0:T(8,128)(2,1)S(1)} %collective-permute-done.refs_1_, bf16[3,2,384,128]{3,2,1,0:T(8,128)(2,1)S(1)} %collective-permute-done.1.refs_2_, ...), custom_call_target="tpu_custom_call" | custom-call | tf_op jit(solution)/shard_map/adam/pallas_call | solution.py:198
  93.6 1.2 %combine.1 = bf16[128,1024]{1,0:T(8,128)(2,1)} custom-call(bf16[128,1024]{1,0:T(8,128)(2,1)S(1)} %table.1.table_ref, bf16[1024,1024]{1,0:T(8,128)(2,1)S(1)} %bitcast.48), custom_call_target="tpu_custom_call" | custom-call | flops 300000000 | bytes 3000000 | tf_op jit(solution)/shard_map/combine/pallas_call | solution.py:224
  (13 shorter events, 0.0 us)
Async XLA Ops:
  12.0 43.6 %copy-start.8 = (bf16[1,2,384,128]{3,2,1,0:T(8,128)(2,1)S(1)}, bf16[1,2,384,128]{3,2,1,0:T(8,128)(2,1)}, u32[]{:S(2)}) copy-start(bf16[1,2,384,128]{3,2,1,0:T(8,128)(2,1)} %get-tuple-element.21) | copy-start | bytes 589828
  12.0 45.6 %copy-start.7 = (bf16[1,2,384,128]{3,2,1,0:T(8,128)(2,1)S(1)}, bf16[1,2,384,128]{3,2,1,0:T(8,128)(2,1)}, u32[]{:S(2)}) copy-start(bf16[1,2,384,128]{3,2,1,0:T(8,128)(2,1)} %get-tuple-element.23) | copy-start | bytes 589828
  12.0 57.5 %copy-start.6 = (bf16[1,2,384,128]{3,2,1,0:T(8,128)(2,1)S(1)}, bf16[1,2,384,128]{3,2,1,0:T(8,128)(2,1)}, u32[]{:S(2)}) copy-start(bf16[1,2,384,128]{3,2,1,0:T(8,128)(2,1)} %get-tuple-element.22) | copy-start | bytes 589828
  12.0 81.5 %all-to-all-start = ((bf16[32,32,1024]{2,1,0:T(8,128)(2,1)}), bf16[32,32,1024]{2,1,0:T(8,128)(2,1)S(1)}, u32[]{:S(2)}, u32[]{:S(2)}) async-start(bf16[32,32,1024]{2,1,0:T(8,128)(2,1)} %bitcast.53), calls=%async_computation | async-start | bytes 4194304 | tf_op jit(solution)/shard_map/all_to_all | solution.py:190
  25.3 47.2 %copy-start.5 = (bf16[1,2,384,128]{3,2,1,0:T(8,128)(2,1)S(1)}, bf16[1,2,384,128]{3,2,1,0:T(8,128)(2,1)}, u32[]{:S(2)}) copy-start(bf16[1,2,384,128]{3,2,1,0:T(8,128)(2,1)} %get-tuple-element.24) | copy-start | bytes 589828
  25.3 59.1 %copy-start.1 = (bf16[1,2,384,128]{3,2,1,0:T(8,128)(2,1)S(1)}, bf16[1,2,384,128]{3,2,1,0:T(8,128)(2,1)}, u32[]{:S(2)}) copy-start(bf16[1,2,384,128]{3,2,1,0:T(8,128)(2,1)} %get-tuple-element.19.refs_3_) | copy-start | bytes 589828
  25.3 63.8 %copy-start.4 = (s32[1,1,960]{2,1,0:T(1,128)S(1)}, s32[1,1,960]{2,1,0:T(1,128)}, u32[]{:S(2)}) copy-start(s32[1,1,960]{2,1,0:T(1,128)} %param.13) | copy-start | bytes 11524
  25.3 30.3 %collective-permute-start = (bf16[3,2,384,128]{3,2,1,0:T(8,128)(2,1)}, bf16[3,2,384,128]{3,2,1,0:T(8,128)(2,1)S(1)}, u32[]{:S(2)}, u32[]{:S(2)}) collective-permute-start(bf16[3,2,384,128]{3,2,1,0:T(8,128)(2,1)} %get-tuple-element.17), channel_id=1, source_target_pairs={{0,2},{1,3},{2,4},{3,5},{4,6},{5,7},{6,8},{7,9},{8,10},{9,11},{10,... | collective-permute-start | bytes 1769480 | tf_op jit(solution)/shard_map/ppermute | solution.py:134
  27.4 30.3 %collective-permute-start.1 = (bf16[3,2,384,128]{3,2,1,0:T(8,128)(2,1)}, bf16[3,2,384,128]{3,2,1,0:T(8,128)(2,1)S(1)}, u32[]{:S(2)}, u32[]{:S(2)}) collective-permute-start(bf16[3,2,384,128]{3,2,1,0:T(8,128)(2,1)} %get-tuple-element.18), channel_id=1, source_target_pairs={{0,22},{1,23},{2,0},{3,1},{4,2},{5,3},{6,4},{7,5},{8,6},{9,7},{10,... | collective-permute-start | bytes 1769480 | tf_op jit(solution)/shard_map/ppermute | solution.py:134
  37.5 18.1 %collective-permute-start.2 = (bf16[1,2,384,128]{3,2,1,0:T(8,128)(2,1)}, bf16[1,2,384,128]{3,2,1,0:T(8,128)(2,1)S(1)}, u32[]{:S(2)}, u32[]{:S(2)}) collective-permute-start(bf16[1,2,384,128]{3,2,1,0:T(8,128)(2,1)} %get-tuple-element.20), channel_id=1, source_target_pairs={{0,4},{1,5},{2,6},{3,7},{4,8},{5,9},{6,10},{7,11},{8,12},{9,13},{1... | collective-permute-start | bytes 589832 | tf_op jit(solution)/shard_map/ppermute | solution.py:134
  55.7 13.8 %collective-permute-start.3 = (bf16[2,384,128]{2,1,0:T(8,128)(2,1)S(1)}, bf16[2,384,128]{2,1,0:T(8,128)(2,1)S(1)}, u32[]{:S(2)}, u32[]{:S(2)}) collective-permute-start(bf16[2,384,128]{2,1,0:T(8,128)(2,1)S(1)} %fusion.2), channel_id=1, source_target_pairs={{0,4},{1,5},{2,6},{3,7},{4,8},{5,9},{6,10},{7,11},{8,12},{9,13},{1... | collective-permute-start | bytes 589832 | tf_op jit(solution)/shard_map/ppermute | solution.py:134
  57.7 14.8 %collective-permute-start.5 = (bf16[2,384,128]{2,1,0:T(8,128)(2,1)S(1)}, bf16[2,384,128]{2,1,0:T(8,128)(2,1)S(1)}, u32[]{:S(2)}, u32[]{:S(2)}) collective-permute-start(bf16[2,384,128]{2,1,0:T(8,128)(2,1)S(1)} %fusion.3), channel_id=1, source_target_pairs={{0,20},{1,21},{2,22},{3,23},{4,0},{5,1},{6,2},{7,3},{8,4},{9,5},{1... | collective-permute-start | bytes 589832 | tf_op jit(solution)/shard_map/ppermute | solution.py:134
  69.6 14.9 %collective-permute-start.4 = (bf16[2,384,128]{2,1,0:T(8,128)(2,1)S(1)}, bf16[2,384,128]{2,1,0:T(8,128)(2,1)S(1)}, u32[]{:S(2)}, u32[]{:S(2)}) collective-permute-start(bf16[2,384,128]{2,1,0:T(8,128)(2,1)S(1)} %fusion.1), channel_id=1, source_target_pairs={{0,4},{1,5},{2,6},{3,7},{4,8},{5,9},{6,10},{7,11},{8,12},{9,13},{1... | collective-permute-start | bytes 589832 | tf_op jit(solution)/shard_map/ppermute | solution.py:134
  72.6 11.8 %collective-permute-start.6 = (bf16[2,384,128]{2,1,0:T(8,128)(2,1)S(1)}, bf16[2,384,128]{2,1,0:T(8,128)(2,1)S(1)}, u32[]{:S(2)}, u32[]{:S(2)}) collective-permute-start(bf16[2,384,128]{2,1,0:T(8,128)(2,1)S(1)} %fusion), channel_id=1, source_target_pairs={{0,20},{1,21},{2,22},{3,23},{4,0},{5,1},{6,2},{7,3},{8,4},{9,5},{1... | collective-permute-start | bytes 589832 | tf_op jit(solution)/shard_map/ppermute | solution.py:134
  84.5 8.0 %collective-permute-start.7 = (bf16[384,128]{1,0:T(8,128)(2,1)S(1)}, bf16[384,128]{1,0:T(8,128)(2,1)S(1)}, u32[]{:S(2)}, u32[]{:S(2)}) collective-permute-start(bf16[384,128]{1,0:T(8,128)(2,1)S(1)} %fusion.4), channel_id=1, source_target_pairs={{0,1},{1,0},{2,3},{3,2},{4,5},{5,4},{6,7},{7,6},{8,9},{9,8},{10,11... | collective-permute-start | bytes 294920 | tf_op jit(solution)/shard_map/ppermute | solution.py:134
  89.1 3.4 %copy-start = (bf16[1,3072,384]{2,1,0:T(8,128)(2,1)S(1)}, bf16[1,3072,384]{2,1,0:T(8,128)(2,1)}, u32[]{:S(2)}) copy-start(bf16[1,3072,384]{2,1,0:T(8,128)(2,1)} %refs_7_.1) | copy-start | bytes 7077892
  89.1 3.4 %copy-start.2 = (f32[1,128,384]{2,1,0:T(8,128)S(1)}, f32[1,128,384]{2,1,0:T(8,128)}, u32[]{:S(2)}) copy-start(f32[1,128,384]{2,1,0:T(8,128)} %refs_8_.1) | copy-start | bytes 589828
  89.1 3.4 %copy-start.3 = (f32[1,128,384]{2,1,0:T(8,128)S(1)}, f32[1,128,384]{2,1,0:T(8,128)}, u32[]{:S(2)}) copy-start(f32[1,128,384]{2,1,0:T(8,128)} %refs_9_.1) | copy-start | bytes 589828

commit v2 on v1

--- a/solution.py
+++ b/solution.py
@@ -18,8 +18,8 @@
 FRAME = 32
 LANES = 128
 
-AHEAD, BEHIND, FAR, KEPT = (5, 3, 1), (-5, -3, -1), (6,), (4, -4, 2, -2, 0)
-GROUPS = (AHEAD, BEHIND, FAR, *((offset,) for offset in KEPT))
+SENT, KEPT = ((5,), (-5,), (6,), (3, 1), (-3, -1)), (4, -4, 2, -2, 0)
+GROUPS = (*SENT, *((offset,) for offset in KEPT))
 
 
 def expert_kernel(narrow_ref, wide_ref, owner_ref, slot_ref, x_hbm, dy_hbm, w_hbm, *refs):
@@ -121,7 +121,9 @@
     out_two[0] = new_two
 
 
-def ring_sum(ahead, behind, far, up_own, down_own, up_next, down_next, own, wide, narrow):
+def ring_sum(
+    ahead, behind, far, ahead_late, behind_late, up_own, down_own, up_next, down_next, own, wide, narrow
+):
     ring = narrow // 2
 
     def hop(value, steps, flip=0):
@@ -142,12 +144,14 @@
     ahead = hop(ahead, 1)
     behind = hop(behind, -1)
     far = hop(far, 2)
+    ahead_late = hop(ahead_late, 1)
+    behind_late = hop(behind_late, -1)
     up = hop(add(far[0], ahead[0], up_own[0]), 2)
     down = hop(add(behind[0], down_own[0]), -2)
-    up = hop(add(up, ahead[1], up_next[0]), 2)
-    down = hop(add(down, behind[1], down_next[0]), -2)
-    across = hop(add(up[1], down[1], ahead[2, 1], behind[2, 1], own[0, 1]), 0, 1)
-    return (ahead, behind, own, up[None], down[None]), (across,)
+    up = hop(add(up, ahead_late[0], up_next[0]), 2)
+    down = hop(add(down, behind_late[0], down_next[0]), -2)
+    across = hop(add(up[1], down[1], ahead_late[1, 1], behind_late[1, 1], own[0, 1]), 0, 1)
+    return (ahead_late, behind_late, own, up[None], down[None]), (across,)
 
 
 def step(weights, act_rows, grad_rows, row_owner, row_slot, slot_token, moment_one, moment_two):

time: 95.2 us -> 87.3 us (0.917)
  the two profiles are of different devices: /device:TPU:8 before, /device:TPU:7 now
where the time goes in v2:
time: 87.3 us; the launch traced here: 86.8 us
  starting transfers between devices  50.4 us (58%)
  waiting for transfers between devices  21.1 us (24%)
  Pallas kernels  14 us (16%)
  between operations  0.92 us (1%)
    ppermute x10, starting transfers between devices, hop(): return lax.ppermute(value, ('wide', 'narrow'), pairs)  41.2 us
    ppermute x10, waiting for transfers between devices, hop(): return lax.ppermute(value, ('wide', 'narrow'), pairs)  21.1 us
    pallas_call x1, Pallas kernels, step(): pl.pallas_call(expert_kernel, out_shape=tuple((jax.ShapeDtypeStruct((n, 2...  11.3 us
    all_to_all x1, starting transfers between devices, step(): lax.all_to_all(outgoing.reshape(wide, FRAME, width), 'wide', split_axis=0...  9.15 us
  transfers between devices with their start and end apart: 11, of which 5 were waited for; matrix products, arithmetic and copies ran while one was open for 0% of the time, Pallas kernels for 2%

profile of v2, /device:TPU:7, one launch (start us, length us, event | category | flops | bytes accessed | tf_op | source)
XLA Modules:
  0.0 86.8 jit_solution(3624448919942051229)
XLA Ops:
  0.6 11.3 %expert.1 = (bf16[1,2,384,128]{3,2,1,0:T(8,128)(2,1)}, bf16[1,2,384,128]{3,2,1,0:T(8,128)(2,1)}, bf16[1,2,384,128]{3,2,1,0:T(8,128)(2,1)}, bf16[2,2,384,128]{3,2...) custom-call(s32[1]{0:T(128)} %bitcast.1.narrow_ref.refs_0_, ...), custom_call_target="tpu_custom_call" | custom-call | flops 7000000000 | bytes 12000000 | tf_op jit(solution)/shard_map/expert/pallas_call | solution.py:171
  12.0 0.0 copy-start.9
  12.0 9.2 %all-to-all-start = ((bf16[32,32,1024]{2,1,0:T(8,128)(2,1)}), bf16[32,32,1024]{2,1,0:T(8,128)(2,1)S(1)}, u32[]{:S(2)}, u32[]{:S(2)}) async-start(bf16[32,32,1024]{2,1,0:T(8,128)(2,1)} %bitcast.53), calls=%async_computation | async-start | bytes 4194304 | tf_op jit(solution)/shard_map/all_to_all | solution.py:194
  21.2 0.0 copy-start.4
  21.2 14.4 %collective-permute-start.2 = (bf16[1,2,384,128]{3,2,1,0:T(8,128)(2,1)}, bf16[1,2,384,128]{3,2,1,0:T(8,128)(2,1)S(1)}, u32[]{:S(2)}, u32[]{:S(2)}) collective-permute-start(bf16[1,2,384,128]{3,2,1,0:T(8,128)(2,1)} %get-tuple-element.22), channel_id=1, source_target_pairs={{0,4},{1,5},{2,6},{3,7},{4,8},{5,9},{6,10},{7,11},{8,12},{9,13},{1... | collective-permute-start | bytes 589832 | tf_op jit(solution)/shard_map/ppermute | solution.py:136
  35.6 2.2 %collective-permute-start.3 = (bf16[1,2,384,128]{3,2,1,0:T(8,128)(2,1)}, bf16[1,2,384,128]{3,2,1,0:T(8,128)(2,1)S(1)}, u32[]{:S(2)}, u32[]{:S(2)}) collective-permute-start(bf16[1,2,384,128]{3,2,1,0:T(8,128)(2,1)} %get-tuple-element.23), channel_id=1, source_target_pairs={{0,2},{1,3},{2,4},{3,5},{4,6},{5,7},{6,8},{7,9},{8,10},{9,11},{10,... | collective-permute-start | bytes 589832 | tf_op jit(solution)/shard_map/ppermute | solution.py:136
  37.8 2.2 %collective-permute-start = (bf16[2,2,384,128]{3,2,1,0:T(8,128)(2,1)}, bf16[2,2,384,128]{3,2,1,0:T(8,128)(2,1)S(1)}, u32[]{:S(2)}, u32[]{:S(2)}) collective-permute-start(bf16[2,2,384,128]{3,2,1,0:T(8,128)(2,1)} %get-tuple-element.19), channel_id=1, source_target_pairs={{0,2},{1,3},{2,4},{3,5},{4,6},{5,7},{6,8},{7,9},{8,10},{9,11},{10,... | collective-permute-start | bytes 1179656 | tf_op jit(solution)/shard_map/ppermute | solution.py:136
  40.0 3.1 %collective-permute-start.6 = (bf16[1,2,384,128]{3,2,1,0:T(8,128)(2,1)S(1)}, bf16[1,2,384,128]{3,2,1,0:T(8,128)(2,1)S(1)}, u32[]{:S(2)}, u32[]{:S(2)}) collective-permute-start(bf16[1,2,384,128]{3,2,1,0:T(8,128)(2,1)S(1)} %copy-done.9), channel_id=1, source_target_pairs={{0,22},{1,23},{2,0},{3,1},{4,2},{5,3},{6,4},{7,5},{8,6},{9,7},{10,... | collective-permute-start | bytes 589832 | tf_op jit(solution)/shard_map/ppermute | solution.py:136
  43.1 3.1 %collective-permute-start.1 = (bf16[2,2,384,128]{3,2,1,0:T(8,128)(2,1)}, bf16[2,2,384,128]{3,2,1,0:T(8,128)(2,1)S(1)}, u32[]{:S(2)}, u32[]{:S(2)}) collective-permute-start(bf16[2,2,384,128]{3,2,1,0:T(8,128)(2,1)} %get-tuple-element.20), channel_id=1, source_target_pairs={{0,22},{1,23},{2,0},{3,1},{4,2},{5,3},{6,4},{7,5},{8,6},{9,7},{10,... | collective-permute-start | bytes 1179656 | tf_op jit(solution)/shard_map/ppermute | solution.py:136
  46.2 0.0 collective-permute-done.2
  46.3 0.1 fusion.2
  46.4 3.4 %collective-permute-start.4 = (bf16[2,384,128]{2,1,0:T(8,128)(2,1)S(1)}, bf16[2,384,128]{2,1,0:T(8,128)(2,1)S(1)}, u32[]{:S(2)}, u32[]{:S(2)}) collective-permute-start(bf16[2,384,128]{2,1,0:T(8,128)(2,1)S(1)} %fusion.2), channel_id=1, source_target_pairs={{0,4},{1,5},{2,6},{3,7},{4,8},{5,9},{6,10},{7,11},{8,12},{9,13},{1... | collective-permute-start | bytes 589832 | tf_op jit(solution)/shard_map/ppermute | solution.py:136
  49.8 0.3 collective-permute-done.6
  50.1 0.1 fusion.3
  50.1 2.5 %collective-permute-start.7 = (bf16[2,384,128]{2,1,0:T(8,128)(2,1)S(1)}, bf16[2,384,128]{2,1,0:T(8,128)(2,1)S(1)}, u32[]{:S(2)}, u32[]{:S(2)}) collective-permute-start(bf16[2,384,128]{2,1,0:T(8,128)(2,1)S(1)} %fusion.3), channel_id=1, source_target_pairs={{0,20},{1,21},{2,22},{3,23},{4,0},{5,1},{6,2},{7,3},{8,4},{9,5},{1... | collective-permute-start | bytes 589832 | tf_op jit(solution)/shard_map/ppermute | solution.py:136
  52.6 5.7 %collective-permute-done.4 = bf16[2,384,128]{2,1,0:T(8,128)(2,1)S(1)} collective-permute-done((bf16[2,384,128]{2,1,0:T(8,128)(2,1)S(1)}, bf16[2,384,128]{2,1,0:T(8,128)(2,1)S(1)}, u32[]{:S(2)}, u32[]{:S(2)}) %collective-permute-start.4) | collective-permute-done | bytes 196640 | tf_op jit(solution)/shard_map/ppermute | solution.py:136
  58.4 0.0 collective-permute-done.refs_1_
  58.4 0.1 fusion.1
  58.5 6.5 %collective-permute-start.5 = (bf16[2,384,128]{2,1,0:T(8,128)(2,1)S(1)}, bf16[2,384,128]{2,1,0:T(8,128)(2,1)S(1)}, u32[]{:S(2)}, u32[]{:S(2)}) collective-permute-start(bf16[2,384,128]{2,1,0:T(8,128)(2,1)S(1)} %fusion.1), channel_id=1, source_target_pairs={{0,4},{1,5},{2,6},{3,7},{4,8},{5,9},{6,10},{7,11},{8,12},{9,13},{1... | collective-permute-start | bytes 589832 | tf_op jit(solution)/shard_map/ppermute | solution.py:136
  65.0 0.1 fusion
  65.1 1.9 %collective-permute-start.8 = (bf16[2,384,128]{2,1,0:T(8,128)(2,1)S(1)}, bf16[2,384,128]{2,1,0:T(8,128)(2,1)S(1)}, u32[]{:S(2)}, u32[]{:S(2)}) collective-permute-start(bf16[2,384,128]{2,1,0:T(8,128)(2,1)S(1)} %fusion), channel_id=1, source_target_pairs={{0,20},{1,21},{2,22},{3,23},{4,0},{5,1},{6,2},{7,3},{8,4},{9,5},{1... | collective-permute-start | bytes 589832 | tf_op jit(solution)/shard_map/ppermute | solution.py:136
  67.0 1.2 %collective-permute-done.5 = bf16[2,384,128]{2,1,0:T(8,128)(2,1)S(1)} collective-permute-done((bf16[2,384,128]{2,1,0:T(8,128)(2,1)S(1)}, bf16[2,384,128]{2,1,0:T(8,128)(2,1)S(1)}, u32[]{:S(2)}, u32[]{:S(2)}) %collective-permute-start.5) | collective-permute-done | bytes 196640 | tf_op jit(solution)/shard_map/ppermute | solution.py:136
  68.2 9.4 %collective-permute-done.8 = bf16[2,384,128]{2,1,0:T(8,128)(2,1)S(1)} collective-permute-done((bf16[2,384,128]{2,1,0:T(8,128)(2,1)S(1)}, bf16[2,384,128]{2,1,0:T(8,128)(2,1)S(1)}, u32[]{:S(2)}, u32[]{:S(2)}) %collective-permute-start.8) | collective-permute-done | bytes 196640 | tf_op jit(solution)/shard_map/ppermute | solution.py:136
  77.7 0.1 fusion.4
  77.7 1.9 %collective-permute-start.9 = (bf16[384,128]{1,0:T(8,128)(2,1)S(1)}, bf16[384,128]{1,0:T(8,128)(2,1)S(1)}, u32[]{:S(2)}, u32[]{:S(2)}) collective-permute-start(bf16[384,128]{1,0:T(8,128)(2,1)S(1)} %fusion.4), channel_id=1, source_target_pairs={{0,1},{1,0},{2,3},{3,2},{4,5},{5,4},{6,7},{7,6},{8,9},{9,8},{10,11... | collective-permute-start | bytes 294920 | tf_op jit(solution)/shard_map/ppermute | solution.py:136
  79.7 0.0 copy-start
  79.7 0.0 copy-start.2
  79.7 0.0 copy-start.3
  79.7 0.5 table.1.table_ref
  80.2 4.4 %collective-permute-done.9.refs_6_ = bf16[384,128]{1,0:T(8,128)(2,1)S(1)} collective-permute-done((bf16[384,128]{1,0:T(8,128)(2,1)S(1)}, bf16[384,128]{1,0:T(8,128)(2,1)S(1)}, u32[]{:S(2)}, u32[]{:S(2)}) %collective-permute-start.9) | collective-permute-done | bytes 98336 | tf_op jit(solution)/shard_map/ppermute | solution.py:136
  84.6 1.0 %adam.1 = (bf16[1,128,384]{2,1,0:T(8,128)(2,1)}, f32[1,128,384]{2,1,0:T(8,128)}, f32[1,128,384]{2,1,0:T(8,128)}) custom-call(s32[1]{0:T(128)} %bitcast.1.narrow_ref.refs_0_, bf16[2,2,384,128]{3,2,1,0:T(8,128)(2,1)S(1)} %collective-permute-done.refs_1_, bf16[2,2,384,128]{3,2,1,0:T(8,128)(2,1)S(1)} %collective-permute-done.1.refs_2_, ...), custom_call_target="tpu_custom_call" | custom-call | tf_op jit(solution)/shard_map/adam/pallas_call | solution.py:202
  85.6 1.2 %combine.1 = bf16[128,1024]{1,0:T(8,128)(2,1)} custom-call(bf16[128,1024]{1,0:T(8,128)(2,1)S(1)} %table.1.table_ref, bf16[1024,1024]{1,0:T(8,128)(2,1)S(1)} %bitcast.48), custom_call_target="tpu_custom_call" | custom-call | flops 300000000 | bytes 3000000 | tf_op jit(solution)/shard_map/combine/pallas_call | solution.py:228
  (19 shorter events, 0.0 us)
Async XLA Ops:
  12.0 28.0 %copy-start.9 = (bf16[1,2,384,128]{3,2,1,0:T(8,128)(2,1)S(1)}, bf16[1,2,384,128]{3,2,1,0:T(8,128)(2,1)}, u32[]{:S(2)}) copy-start(bf16[1,2,384,128]{3,2,1,0:T(8,128)(2,1)} %get-tuple-element.26) | copy-start | bytes 589828
  12.0 34.3 %copy-start.8 = (bf16[1,2,384,128]{3,2,1,0:T(8,128)(2,1)S(1)}, bf16[1,2,384,128]{3,2,1,0:T(8,128)(2,1)}, u32[]{:S(2)}) copy-start(bf16[1,2,384,128]{3,2,1,0:T(8,128)(2,1)} %get-tuple-element.24) | copy-start | bytes 589828
  12.0 38.1 %copy-start.7 = (bf16[1,2,384,128]{3,2,1,0:T(8,128)(2,1)S(1)}, bf16[1,2,384,128]{3,2,1,0:T(8,128)(2,1)}, u32[]{:S(2)}) copy-start(bf16[1,2,384,128]{3,2,1,0:T(8,128)(2,1)} %get-tuple-element.27) | copy-start | bytes 589828
  12.0 46.4 %copy-start.6 = (bf16[1,2,384,128]{3,2,1,0:T(8,128)(2,1)S(1)}, bf16[1,2,384,128]{3,2,1,0:T(8,128)(2,1)}, u32[]{:S(2)}) copy-start(bf16[1,2,384,128]{3,2,1,0:T(8,128)(2,1)} %get-tuple-element.25) | copy-start | bytes 589828
  12.0 73.6 %all-to-all-start = ((bf16[32,32,1024]{2,1,0:T(8,128)(2,1)}), bf16[32,32,1024]{2,1,0:T(8,128)(2,1)S(1)}, u32[]{:S(2)}, u32[]{:S(2)}) async-start(bf16[32,32,1024]{2,1,0:T(8,128)(2,1)} %bitcast.53), calls=%async_computation | async-start | bytes 4194304 | tf_op jit(solution)/shard_map/all_to_all | solution.py:194
  21.2 43.8 %copy-start.5 = (bf16[1,2,384,128]{3,2,1,0:T(8,128)(2,1)S(1)}, bf16[1,2,384,128]{3,2,1,0:T(8,128)(2,1)}, u32[]{:S(2)}) copy-start(bf16[1,2,384,128]{3,2,1,0:T(8,128)(2,1)} %get-tuple-element.28) | copy-start | bytes 589828
  21.2 56.5 %copy-start.1 = (bf16[1,2,384,128]{3,2,1,0:T(8,128)(2,1)S(1)}, bf16[1,2,384,128]{3,2,1,0:T(8,128)(2,1)}, u32[]{:S(2)}) copy-start(bf16[1,2,384,128]{3,2,1,0:T(8,128)(2,1)} %get-tuple-element.21.refs_3_) | copy-start | bytes 589828
  21.2 58.5 %copy-start.4 = (s32[1,1,960]{2,1,0:T(1,128)S(1)}, s32[1,1,960]{2,1,0:T(1,128)}, u32[]{:S(2)}) copy-start(s32[1,1,960]{2,1,0:T(1,128)} %param.13) | copy-start | bytes 11524
  21.2 25.0 %collective-permute-start.2 = (bf16[1,2,384,128]{3,2,1,0:T(8,128)(2,1)}, bf16[1,2,384,128]{3,2,1,0:T(8,128)(2,1)S(1)}, u32[]{:S(2)}, u32[]{:S(2)}) collective-permute-start(bf16[1,2,384,128]{3,2,1,0:T(8,128)(2,1)} %get-tuple-element.22), channel_id=1, source_target_pairs={{0,4},{1,5},{2,6},{3,7},{4,8},{5,9},{6,10},{7,11},{8,12},{9,13},{1... | collective-permute-start | bytes 589832 | tf_op jit(solution)/shard_map/ppermute | solution.py:136
  35.6 10.6 %collective-permute-start.3 = (bf16[1,2,384,128]{3,2,1,0:T(8,128)(2,1)}, bf16[1,2,384,128]{3,2,1,0:T(8,128)(2,1)S(1)}, u32[]{:S(2)}, u32[]{:S(2)}) collective-permute-start(bf16[1,2,384,128]{3,2,1,0:T(8,128)(2,1)} %get-tuple-element.23), channel_id=1, source_target_pairs={{0,2},{1,3},{2,4},{3,5},{4,6},{5,7},{6,8},{7,9},{8,10},{9,11},{10,... | collective-permute-start | bytes 589832 | tf_op jit(solution)/shard_map/ppermute | solution.py:136
  37.8 20.5 %collective-permute-start = (bf16[2,2,384,128]{3,2,1,0:T(8,128)(2,1)}, bf16[2,2,384,128]{3,2,1,0:T(8,128)(2,1)S(1)}, u32[]{:S(2)}, u32[]{:S(2)}) collective-permute-start(bf16[2,2,384,128]{3,2,1,0:T(8,128)(2,1)} %get-tuple-element.19), channel_id=1, source_target_pairs={{0,2},{1,3},{2,4},{3,5},{4,6},{5,7},{6,8},{7,9},{8,10},{9,11},{10,... | collective-permute-start | bytes 1179656 | tf_op jit(solution)/shard_map/ppermute | solution.py:136
  40.0 10.0 %collective-permute-start.6 = (bf16[1,2,384,128]{3,2,1,0:T(8,128)(2,1)S(1)}, bf16[1,2,384,128]{3,2,1,0:T(8,128)(2,1)S(1)}, u32[]{:S(2)}, u32[]{:S(2)}) collective-permute-start(bf16[1,2,384,128]{3,2,1,0:T(8,128)(2,1)S(1)} %copy-done.9), channel_id=1, source_target_pairs={{0,22},{1,23},{2,0},{3,1},{4,2},{5,3},{6,4},{7,5},{8,6},{9,7},{10,... | collective-permute-start | bytes 589832 | tf_op jit(solution)/shard_map/ppermute | solution.py:136
  43.1 21.8 %collective-permute-start.1 = (bf16[2,2,384,128]{3,2,1,0:T(8,128)(2,1)}, bf16[2,2,384,128]{3,2,1,0:T(8,128)(2,1)S(1)}, u32[]{:S(2)}, u32[]{:S(2)}) collective-permute-start(bf16[2,2,384,128]{3,2,1,0:T(8,128)(2,1)} %get-tuple-element.20), channel_id=1, source_target_pairs={{0,22},{1,23},{2,0},{3,1},{4,2},{5,3},{6,4},{7,5},{8,6},{9,7},{10,... | collective-permute-start | bytes 1179656 | tf_op jit(solution)/shard_map/ppermute | solution.py:136
  46.4 12.0 %collective-permute-start.4 = (bf16[2,384,128]{2,1,0:T(8,128)(2,1)S(1)}, bf16[2,384,128]{2,1,0:T(8,128)(2,1)S(1)}, u32[]{:S(2)}, u32[]{:S(2)}) collective-permute-start(bf16[2,384,128]{2,1,0:T(8,128)(2,1)S(1)} %fusion.2), channel_id=1, source_target_pairs={{0,4},{1,5},{2,6},{3,7},{4,8},{5,9},{6,10},{7,11},{8,12},{9,13},{1... | collective-permute-start | bytes 589832 | tf_op jit(solution)/shard_map/ppermute | solution.py:136
  50.1 14.9 %collective-permute-start.7 = (bf16[2,384,128]{2,1,0:T(8,128)(2,1)S(1)}, bf16[2,384,128]{2,1,0:T(8,128)(2,1)S(1)}, u32[]{:S(2)}, u32[]{:S(2)}) collective-permute-start(bf16[2,384,128]{2,1,0:T(8,128)(2,1)S(1)} %fusion.3), channel_id=1, source_target_pairs={{0,20},{1,21},{2,22},{3,23},{4,0},{5,1},{6,2},{7,3},{8,4},{9,5},{1... | collective-permute-start | bytes 589832 | tf_op jit(solution)/shard_map/ppermute | solution.py:136
  58.5 9.8 %collective-permute-start.5 = (bf16[2,384,128]{2,1,0:T(8,128)(2,1)S(1)}, bf16[2,384,128]{2,1,0:T(8,128)(2,1)S(1)}, u32[]{:S(2)}, u32[]{:S(2)}) collective-permute-start(bf16[2,384,128]{2,1,0:T(8,128)(2,1)S(1)} %fusion.1), channel_id=1, source_target_pairs={{0,4},{1,5},{2,6},{3,7},{4,8},{5,9},{6,10},{7,11},{8,12},{9,13},{1... | collective-permute-start | bytes 589832 | tf_op jit(solution)/shard_map/ppermute | solution.py:136
  65.1 12.6 %collective-permute-start.8 = (bf16[2,384,128]{2,1,0:T(8,128)(2,1)S(1)}, bf16[2,384,128]{2,1,0:T(8,128)(2,1)S(1)}, u32[]{:S(2)}, u32[]{:S(2)}) collective-permute-start(bf16[2,384,128]{2,1,0:T(8,128)(2,1)S(1)} %fusion), channel_id=1, source_target_pairs={{0,20},{1,21},{2,22},{3,23},{4,0},{5,1},{6,2},{7,3},{8,4},{9,5},{1... | collective-permute-start | bytes 589832 | tf_op jit(solution)/shard_map/ppermute | solution.py:136
  77.7 6.9 %collective-permute-start.9 = (bf16[384,128]{1,0:T(8,128)(2,1)S(1)}, bf16[384,128]{1,0:T(8,128)(2,1)S(1)}, u32[]{:S(2)}, u32[]{:S(2)}) collective-permute-start(bf16[384,128]{1,0:T(8,128)(2,1)S(1)} %fusion.4), channel_id=1, source_target_pairs={{0,1},{1,0},{2,3},{3,2},{4,5},{5,4},{6,7},{7,6},{8,9},{9,8},{10,11... | collective-permute-start | bytes 294920 | tf_op jit(solution)/shard_map/ppermute | solution.py:136
  79.7 4.9 %copy-start = (bf16[1,3072,384]{2,1,0:T(8,128)(2,1)S(1)}, bf16[1,3072,384]{2,1,0:T(8,128)(2,1)}, u32[]{:S(2)}) copy-start(bf16[1,3072,384]{2,1,0:T(8,128)(2,1)} %refs_7_.1) | copy-start | bytes 7077892
  79.7 4.9 %copy-start.2 = (f32[1,128,384]{2,1,0:T(8,128)S(1)}, f32[1,128,384]{2,1,0:T(8,128)}, u32[]{:S(2)}) copy-start(f32[1,128,384]{2,1,0:T(8,128)} %refs_8_.1) | copy-start | bytes 589828
  79.7 4.9 %copy-start.3 = (f32[1,128,384]{2,1,0:T(8,128)S(1)}, f32[1,128,384]{2,1,0:T(8,128)}, u32[]{:S(2)}) copy-start(f32[1,128,384]{2,1,0:T(8,128)} %refs_9_.1) | copy-start | bytes 589828
